TPU v7x, 128 devices: a whole 4x4x4 slice. The times are simulated.
128 devices in a mesh: leaf: 16 (over x, y_lo, core), panel: 8 (over z, y_hi).
Axes of the slice: x: 4, y: 4 (y_hi: 2, y_lo: 2; y = y_hi * 2 + y_lo), z: 4, core: 2. Of those that a mesh axis runs over, the one named last changes fastest.
Arguments:
- ext_rows: bfloat16 [16, 4608, 5120], P('leaf', 'panel'), as said below
- iface_rows: bfloat16 [16, 512, 5120], P('leaf', 'panel'), as said below
- inverse: bfloat16 [16, 512, 512], P('leaf', 'panel'), as said below
- pivot: int32 [16, 256], P('leaf'), may hold values from 0 to 255, as said below
- flags: int32 [16, 9], P('leaf'), may hold values 0 or 1
Outputs:
- merged: bfloat16 [16, 4608, 9216], P('leaf', 'panel')
Inputs may be any that keep to these rules, and one draw needn't show every extreme that they name: `pivot`: each row is a permutation of 0 to 255; the rows of two merge partners are inverse to each other. `ext_rows`: each 2 x 2 block of real entries is the real form [[a, -b], [b, a]] of one complex number. `iface_rows`: each 2 x 2 block of real entries is the real form [[a, -b], [b, a]] of one complex number. `inverse`: each 2 x 2 block of real entries is the real form [[a, -b], [b, a]] of one complex number.
All inputs are finite; a program needn't handle non-finite values. No bound on the sum of `flags` on one device may be relied on, other than what follows from the above.
Results may differ from a plain program's by a relative error of at most 0.005.
Values may be sent and summed in bfloat16 or wider, within the bound.
No kernel may reach another device: no remote copies, remote signals or barrier semaphores. Data moves between devices by JAX's collectives and lax.ppermute only.
A program may use at most 128 MiB of HBM per device.

v0:
```python
import jax
import jax.numpy as jnp
from jax import lax
from jax.sharding import PartitionSpec as P

FPTS = 256
BIT = 2


def partner(array, axis, bit):
    return lax.ppermute(array, axis, [(i, i ^ 1 << bit) for i in range(lax.axis_size(axis))])


def per_device(ext_rows, iface_rows, inverse, pivot, flags):
    ext = ext_rows[0]
    iface = iface_rows[0]
    winv = inverse[0]
    idim = winv.shape[1]
    edim = ext.shape[1] - idim
    rows = ext.shape[0]
    direct_block = ext[:, :edim]
    ext_to_iface = ext[:, edim:]
    own_outward = iface[:, :edim]
    own_inward = iface[:, edim:]
    order = (2 * pivot[0][:, None] + jnp.arange(2, dtype=jnp.int32)[None, :]).reshape(-1)
    back = jnp.argsort(order)
    permuted = jnp.take(winv, back, axis=1)
    coupled = jnp.dot(
        ext_to_iface,
        lax.all_gather(permuted, "panel", axis=0, tiled=True),
        preferred_element_type=jnp.float32,
    ).astype(jnp.bfloat16)
    inward_send = lax.all_gather(own_inward, "panel", axis=0, tiled=True)
    partner_inward, partner_outward = partner((inward_send, own_outward), "leaf", BIT)
    through = jnp.dot(
        coupled, jnp.take(partner_inward, order, axis=1), preferred_element_type=jnp.float32
    )
    through = through.astype(jnp.bfloat16)
    own_sum = jnp.dot(
        through,
        lax.all_gather(own_outward, "panel", axis=0, tiled=True),
        preferred_element_type=jnp.float32,
    )
    cross_sum = jnp.dot(
        coupled,
        lax.all_gather(partner_outward, "panel", axis=0, tiled=True),
        preferred_element_type=jnp.float32,
    )
    cross = cross_sum.astype(jnp.bfloat16)
    own = direct_block.astype(jnp.float32) + own_sum
    row_index = lax.axis_index("panel") * rows + jnp.arange(rows, dtype=jnp.int32)
    face_index = row_index // (2 * FPTS)
    faces = flags.shape[1]
    matches = (face_index[:, None] == jnp.arange(faces, dtype=jnp.int32)[None, :]).astype(
        jnp.float32
    )
    opened = jnp.sum(matches * flags[0][None, :].astype(jnp.float32), axis=1)
    sign = 1.0 - 2.0 * opened
    whole = jnp.concatenate([own, cross.astype(jnp.float32)], axis=1)
    return (sign[:, None] * whole).astype(jnp.bfloat16)[None]


def solution(mesh):
    placed = (
        P("leaf", "panel", None),
        P("leaf", "panel", None),
        P("leaf", "panel", None),
        P("leaf", None),
        P("leaf", None),
    )
    return jax.shard_map(
        per_device, mesh=mesh, in_specs=placed, out_specs=P("leaf", "panel", None), check_vma=False
    )
```

profile of v0, /device:TPU:0, one launch (start us, length us, event | category | flops | bytes accessed | tf_op | source)
XLA Modules:
  0.0 188.1 jit_solution(17509091723812896710)
XLA Ops:
  6.5 0.0 all-gather.3.cloned.1.call-start
  6.5 1.9 %slice.23 = bf16[64,4608]{1,0:T(8,128)(2,1)} slice(bf16[64,5120]{1,0:T(8,128)(2,1)} %bitcast.22), slice={[0:64], [0:4608]} | slice | bytes 1179648 | tf_op jit(solution)/shard_map/slice | solution.py:23
  8.5 0.0 all-gather.3.cloned.1.call-update
  8.5 0.0 all-gather.5.cloned.1.call-start
  8.5 1.7 collective-permute-start.1
  10.2 13.5 %collective-permute-done.1 = bf16[64,4608]{1,0:T(8,128)(2,1)S(1)} collective-permute-done((bf16[64,4608]{1,0:T(8,128)(2,1)}, bf16[64,4608]{1,0:T(8,128)(2,1)S(1)}, u32[]{:S(2)}, u32[]{:S(2)}) %collective-permute-start.1) | collective-permute-done | bytes 589856 | tf_op jit(solution)/shard_map/ppermute | solution.py:11
  23.7 0.0 copy-start.1
  23.7 0.8 copy-done.1
  24.6 0.0 all-gather.5.cloned.1.call-update
  24.6 0.8 slice.22
  25.4 39.8 %all_gather.13 = bf16[512,512]{1,0:T(8,128)(2,1)S(1)} all-gather(bf16[64,512]{1,0:T(8,128)(2,1)S(1)} %slice.22), channel_id=1, replica_groups=mesh['leaf'=16,'panel'=8] {'panel'}, dimensions={0}, use_global_device_ids=true | all-gather | bytes 589824 | tf_op jit(solution)/shard_map/all_gather | solution.py:33
  65.2 0.2 copy.15
  65.4 1.6 collective-permute-start
  67.0 0.7 broadcast_multiply_fusion
  67.7 0.1 iota_add_fusion
  67.8 0.1 add.79
  67.9 0.1 add.83
  68.0 1.0 copy.13
  69.0 3.8 %sort.17 = (s32[512]{0:T(512)}, s32[512]{0:T(512)S(1)}) sort(s32[512]{0:T(512)S(1)} %add.79, s32[512]{0:T(512)S(1)} %iota.18), dimensions={0}, to_apply=%region_1.2 | sort | flops 4608 | bytes 8192 | tf_op jit(solution)/shard_map/jit(argsort)/sort | solution.py:26
  72.8 1.3 gather_fusion
  74.2 0.7 convert_bitcast_fusion
  74.8 0.1 select_reduce_fusion
  75.0 0.1 select_bitcast_fusion
  75.1 0.1 copy.14
  75.2 36.9 %all_gather.12 = bf16[512,512]{1,0:T(8,128)(2,1)S(1)} all-gather(bf16[64,512]{1,0:T(8,128)(2,1)S(1)} %copy.14), channel_id=1, replica_groups=mesh['leaf'=16,'panel'=8] {'panel'}, dimensions={0}, use_global_device_ids=true | all-gather | bytes 589824 | tf_op jit(solution)/shard_map/all_gather | solution.py:30
  112.1 1.5 convolution_convert_fusion.1
  113.7 0.0 collective-permute-done
  113.7 2.0 %gather_fusion.1 = bf16[512,512]{1,0:T(8,128)(2,1)S(1)} fusion(bf16[512,512]{0,1:T(8,128)(2,1)S(1)} %collective-permute-done, s32[1024]{0:T(1024)S(1)} %pad_clamp_fusion), kind=kCustom, calls=%fused_computation.1 | custom fusion | bytes 1050624 | tf_op jit(solution)/shard_map/jit(_take)/gather | solution.py:36
  115.6 0.0 all-gather.3.cloned.1.call-done
  115.7 9.3 %add_bitcast_fusion = f32[1,576,4608]{2,1,0:T(8,128)} fusion(bf16[512,4608]{1,0:T(8,128)(2,1)} %all-gather.3.cloned.1.call-done, bf16[576,5120]{1,0:T(8,128)(2,1)} %bitcast.27, bf16[512,576]{0,1:T(8,128)(2,1)S(1)} %convolution_convert_fusion.1, bf16[512,512]{1,0:T(8,128)(2,1)S(1)} %gather_fusion.1, pred[512]{0:T(512)(128)(4,1)S(1)} %compare_and_fusion), kind=kOutput, calls=%fused_computation.4 | convolution fusion | flops 3025764352 | bytes 21758464 | tf_op jit(solution)/shard_map/dot_general | solution.py:39
  125.0 45.7 %all-gather.5.cloned.1.call-done = bf16[512,4608]{1,0:T(8,128)(2,1)} async-done(((bf16[64,4608]{1,0:T(8,128)(2,1)}), bf16[512,4608]{1,0:T(8,128)(2,1)}) %all-gather.5.cloned.1.call-update) | async-done | bytes 4718608 | tf_op jit(solution)/shard_map/all_gather | solution.py:46
  170.7 0.0 copy-start
  170.7 4.9 %fusion.2 = f32[1,576,4608]{2,1,0:T(8,128)S(1)} fusion(bf16[512,576]{0,1:T(8,128)(2,1)S(1)} %convolution_convert_fusion.1, bf16[512,4608]{1,0:T(8,128)(2,1)} %all-gather.5.cloned.1.call-done), kind=kOutput, calls=%fused_computation.7 | convolution fusion | flops 2723217408 | bytes 15925248 | tf_op jit(solution)/shard_map/dot_general | solution.py:44
  175.7 0.5 copy-done
  176.1 5.1 %fusion = bf16[1,576,9216]{2,1,0:T(8,128)(2,1)} fusion(f32[1,576,4608]{2,1,0:T(8,128)S(1)} %fusion.2, f32[1,576,4608]{2,1,0:T(8,128)S(1)} %copy-done, f32[576]{0:T(1024)S(1)} %multiply_subtract_fusion), kind=kLoop, calls=%fused_computation.3 | loop fusion | flops 15925248 | bytes 31852800 | tf_op jit(solution)/shard_map/convert_element_type | solution.py:60
  (9 shorter events, 0.1 us)
Async XLA Ops:
  6.5 109.1 %all-gather.3.cloned.1.call-start = ((), (), s32[]{:S(2)}) async-start(), calls=%async_computation | async-start | bytes 5308416 | tf_op jit(solution)/shard_map/all_gather | solution.py:41
  8.5 162.2 %all-gather.5.cloned.1.call-start = ((), (), s32[]{:S(2)}) async-start(), calls=%async_computation.1 | async-start | bytes 5308416 | tf_op jit(solution)/shard_map/all_gather | solution.py:46
  8.5 15.2 %collective-permute-start.1 = (bf16[64,4608]{1,0:T(8,128)(2,1)}, bf16[64,4608]{1,0:T(8,128)(2,1)S(1)}, u32[]{:S(2)}, u32[]{:S(2)}) collective-permute-start(bf16[64,4608]{1,0:T(8,128)(2,1)} %slice.23), channel_id=1, source_target_pairs={{0,32},{8,40},{16,48},{24,56},{32,0},{40,8},{48,16},{56,24},{64,96... | collective-permute-start | bytes 1769480 | tf_op jit(solution)/shard_map/ppermute | solution.py:11
  23.7 0.8 copy-start.1
  65.4 48.3 %collective-permute-start = (bf16[512,512]{0,1:T(8,128)(2,1)S(1)}, bf16[512,512]{0,1:T(8,128)(2,1)S(1)}, u32[]{:S(2)}, u32[]{:S(2)}) collective-permute-start(bf16[512,512]{0,1:T(8,128)(2,1)S(1)} %copy.15), channel_id=1, source_target_pairs={{0,32},{8,40},{16,48},{24,56},{32,0},{40,8},{48,16},{56,24},{64,96... | collective-permute-start | bytes 1572872 | tf_op jit(solution)/shard_map/ppermute | solution.py:11
  170.7 5.4 %copy-start = (f32[1,576,4608]{2,1,0:T(8,128)S(1)}, f32[1,576,4608]{2,1,0:T(8,128)}, u32[]{:S(2)}) copy-start(f32[1,576,4608]{2,1,0:T(8,128)} %add_bitcast_fusion) | copy-start | bytes 31850500
Sparse Core Ops, SparseCore 0:
  9.6 84.3 all-gather.2
  96.3 74.3 all-gather.4
where the time goes:
time: 188 us
  blocking collectives  76.6 us (41%)
  waiting for transfers between devices  59.3 us (32%)
  matrix products  15.8 us (8%)
  between operations  13.5 us (7%)
  other arithmetic  10.6 us (6%)
  local copies, waits for them, and re-layouts  8.93 us (5%)
  starting transfers between devices  3.29 us (2%)
    all_gather x1, waiting for transfers between devices, per_device(): lax.all_gather(partner_outward, 'panel', axis=0, tiled=True)  45.7 us
    all_gather x1, blocking collectives, per_device(): inward_send = lax.all_gather(own_inward, 'panel', axis=0, tiled=True)  39.8 us
    all_gather x1, blocking collectives, per_device(): lax.all_gather(permuted, 'panel', axis=0, tiled=True)  36.9 us
    ppermute x2, waiting for transfers between devices, partner(): lax.ppermute(array, axis, [(i, i ^ 1 << bit) for i in range(lax.axis_size...  13.5 us
    dot_general x1, matrix products, per_device(): jnp.dot(through, lax.all_gather(own_outward, 'panel', axis=0, tiled=True)...  9.34 us
    convert_element_type x1, other arithmetic, per_device(): return (sign[:, None] * whole).astype(jnp.bfloat16)[None]  5.09 us
    dot_general x1, matrix products, per_device(): jnp.dot(coupled, lax.all_gather(partner_outward, 'panel', axis=0, tiled=T...  4.93 us
    sort x1, other arithmetic, per_device(): back = jnp.argsort(order)  3.78 us
  transfers between devices with their start and end apart: 4, of which 2 were waited for; matrix products, arithmetic and copies ran while one was open for 12% of the time, Pallas kernels for 0%

commit v1 on v0

--- a/solution.py
+++ b/solution.py
@@ -2,9 +2,16 @@
 import jax.numpy as jnp
 from jax import lax
 from jax.sharding import PartitionSpec as P
+from jax.lax import all_to_all, axis_size
 
 FPTS = 256
 BIT = 2
+
+
+def build_the_plane(target, dim_no):
+    return jnp.concatenate(
+        all_to_all(jnp.stack([target] * axis_size("panel"), 0), "panel", 0, 0), dim_no
+    )
 
 
 def partner(array, axis, bit):
@@ -42,9 +49,7 @@
         preferred_element_type=jnp.float32,
     )
     cross_sum = jnp.dot(
-        coupled,
-        lax.all_gather(partner_outward, "panel", axis=0, tiled=True),
-        preferred_element_type=jnp.float32,
+        coupled, build_the_plane(partner_outward, dim_no=0), preferred_element_type=jnp.float32
     )
     cross = cross_sum.astype(jnp.bfloat16)
     own = direct_block.astype(jnp.float32) + own_sum

time: 188 us -> 228 us (1.21)
  blocking collectives: 76.6 us -> 145 us
  waiting for transfers between devices: 59.3 us -> 13.6 us
  starting transfers between devices: 3.29 us -> 11.6 us
  other arithmetic: 10.6 us -> 16.1 us
  matrix products: 15.8 us -> 18.6 us
    all_gather x1, blocking collectives: 39.8 us -> 110 us  [per_device(): inward_send = lax.all_gather(own_inward, 'panel', axis=0, tiled=True)]
    all_gather x1 -> x0, waiting for transfers between devices: 45.7 us -> none  [per_device(): lax.all_gather(partner_outward, 'panel', axis=0, tiled=True)]
    all_to_all x0 -> x1, starting transfers between devices: none -> 8.33 us  [build_the_plane(): all_to_all(jnp.stack([target] * axis_size('panel'), 0), 'panel', 0, 0)]
    convert_element_type x1, other arithmetic: 5.09 us -> 11.9 us  [per_device(): return (sign[:, None] * whole).astype(jnp.bfloat16)[None]]
    dot_general x1, matrix products: 4.93 us -> 7.91 us  [per_device(): jnp.dot(coupled, build_the_plane(partner_outward, dim_no=0), preferred_el...]
    another operation x0 -> x1, local copies, waits for them, and re-layouts: none -> 2.57 us  [build_the_plane(): jnp.stack([target] * axis_size('panel'), 0)]
  transfers between devices with their start and end apart: 4 -> 4, of which waited for: 2 -> 1; matrix products, arithmetic and copies ran while one was open for 12% -> 9% of each run, Pallas kernels for 0% -> 0%
where the time goes in v1:
time: 228 us
  blocking collectives  145 us (64%)
  matrix products  18.6 us (8%)
  other arithmetic  16.1 us (7%)
  waiting for transfers between devices  13.6 us (6%)
  between operations  13.6 us (6%)
  starting transfers between devices  11.6 us (5%)
  local copies, waits for them, and re-layouts  9.37 us (4%)
    all_gather x1, blocking collectives, per_device(): inward_send = lax.all_gather(own_inward, 'panel', axis=0, tiled=True)  110 us
    all_gather x1, blocking collectives, per_device(): lax.all_gather(permuted, 'panel', axis=0, tiled=True)  35.4 us
    ppermute x2, waiting for transfers between devices, partner(): lax.ppermute(array, axis, [(i, i ^ 1 << bit) for i in range(lax.axis_size...  13.5 us
    convert_element_type x1, other arithmetic, per_device(): return (sign[:, None] * whole).astype(jnp.bfloat16)[None]  11.9 us
    dot_general x1, matrix products, per_device(): jnp.dot(through, lax.all_gather(own_outward, 'panel', axis=0, tiled=True)...  9.18 us
    all_to_all x1, starting transfers between devices, build_the_plane(): all_to_all(jnp.stack([target] * axis_size('panel'), 0), 'panel', 0, 0)  8.33 us
    dot_general x1, matrix products, per_device(): jnp.dot(coupled, build_the_plane(partner_outward, dim_no=0), preferred_el...  7.91 us
  transfers between devices with their start and end apart: 4, of which 1 were waited for; matrix products, arithmetic and copies ran while one was open for 9% of the time, Pallas kernels for 0%

profile of v1, /device:TPU:0, one launch (start us, length us, event | category | flops | bytes accessed | tf_op | source)
XLA Modules:
  0.0 227.8 jit_solution(5612745478613453591)
XLA Ops:
  6.5 0.0 all-gather.2.cloned.1.call-start
  6.5 1.9 slice.23
  8.5 0.0 all-gather.2.cloned.1.call-update
  8.5 1.7 collective-permute-start.1
  10.2 13.5 %collective-permute-done.1 = bf16[64,4608]{1,0:T(8,128)(2,1)S(1)} collective-permute-done((bf16[64,4608]{1,0:T(8,128)(2,1)}, bf16[64,4608]{1,0:T(8,128)(2,1)S(1)}, u32[]{:S(2)}, u32[]{:S(2)}) %collective-permute-start.1) | collective-permute-done | bytes 589856 | tf_op jit(solution)/shard_map/ppermute | solution.py:18
  23.7 2.6 %stack.2 = bf16[8,64,4608]{2,1,0:T(8,128)(2,1)} broadcast(bf16[64,4608]{1,0:T(8,128)(2,1)S(1)} %collective-permute-done.1), dimensions={1,2} | broadcast | bytes 5308416 | tf_op jit(solution)/shard_map/stack | solution.py:13
  26.3 0.0 copy-start.1
  26.3 0.0 copy-start
  26.3 0.0 copy-start.2
  26.3 8.3 %all-to-all-start = ((bf16[8,64,4608]{2,1,0:T(8,128)(2,1)}), bf16[8,64,4608]{2,1,0:T(8,128)(2,1)}, u32[]{:S(2)}, u32[]{:S(2)}) async-start(bf16[8,64,4608]{2,1,0:T(8,128)(2,1)} %stack.2), calls=%async_computation | async-start | bytes 9437184 | tf_op jit(solution)/shard_map/all_to_all | solution.py:13
  34.6 0.8 slice.22
  35.5 109.7 %all_gather.10 = bf16[512,512]{1,0:T(8,128)(2,1)S(1)} all-gather(bf16[64,512]{1,0:T(8,128)(2,1)S(1)} %slice.22), channel_id=1, replica_groups=mesh['leaf'=16,'panel'=8] {'panel'}, dimensions={0}, use_global_device_ids=true | all-gather | bytes 589824 | tf_op jit(solution)/shard_map/all_gather | solution.py:40
  145.1 0.2 copy.17
  145.4 1.6 collective-permute-start
  147.0 0.0 copy-done.1
  147.0 0.1 iota_add_fusion
  147.1 0.1 add.79
  147.2 0.1 add.83
  147.4 0.0 copy-done
  147.4 0.1 copy.15
  147.5 3.8 %sort.17 = (s32[512]{0:T(512)}, s32[512]{0:T(512)S(1)}) sort(s32[512]{0:T(512)S(1)} %add.79, s32[512]{0:T(512)S(1)} %iota.18), dimensions={0}, to_apply=%region_1.2 | sort | flops 4608 | bytes 8192 | tf_op jit(solution)/shard_map/jit(argsort)/sort | solution.py:33
  151.3 1.3 gather_fusion
  152.6 0.0 copy-done.2
  152.7 0.1 select_reduce_fusion
  152.8 0.1 select_bitcast_fusion
  153.0 0.1 copy.16
  153.1 35.4 %all_gather.9 = bf16[512,512]{1,0:T(8,128)(2,1)S(1)} all-gather(bf16[64,512]{1,0:T(8,128)(2,1)S(1)} %copy.16), channel_id=1, replica_groups=mesh['leaf'=16,'panel'=8] {'panel'}, dimensions={0}, use_global_device_ids=true | all-gather | bytes 589824 | tf_op jit(solution)/shard_map/all_gather | solution.py:37
  188.4 1.5 convolution_convert_fusion.1
  190.0 0.0 collective-permute-done
  190.0 2.0 gather_fusion.1
  192.0 0.0 all-to-all-done
  192.0 7.9 %fusion.2 = f32[1,576,4608]{2,1,0:T(8,128)} fusion(bf16[512,576]{0,1:T(8,128)(2,1)S(1)} %convolution_convert_fusion.1, bf16[512,4608]{1,0:T(8,128)(2,1)} %bitcast.8), kind=kOutput, calls=%fused_computation.7 | convolution fusion | flops 2723217408 | bytes 15925248 | tf_op jit(solution)/shard_map/dot_general | solution.py:51
  199.9 0.0 all-gather.2.cloned.1.call-done
  199.9 9.2 %add_bitcast_fusion = f32[1,576,4608]{2,1,0:T(8,128)} fusion(bf16[512,4608]{1,0:T(8,128)(2,1)} %all-gather.2.cloned.1.call-done, bf16[576,5120]{1,0:T(8,128)(2,1)} %bitcast.28, bf16[512,576]{0,1:T(8,128)(2,1)S(1)} %convolution_convert_fusion.1, bf16[512,512]{1,0:T(8,128)(2,1)S(1)} %gather_fusion.1, pred[512]{0:T(512)(128)(4,1)S(1)} %compare_and_fusion), kind=kOutput, calls=%fused_computation.4 | convolution fusion | flops 3025764352 | bytes 21758464 | tf_op jit(solution)/shard_map/dot_general | solution.py:46
  209.1 11.9 %fusion = bf16[1,576,9216]{2,1,0:T(8,128)(2,1)} fusion(f32[1,576,4608]{2,1,0:T(8,128)} %fusion.2, f32[1,576,4608]{2,1,0:T(8,128)} %add_bitcast_fusion, f32[576]{0:T(1024)S(1)} %multiply_subtract_fusion), kind=kLoop, calls=%fused_computation.3 | loop fusion | flops 15925248 | bytes 31852800 | tf_op jit(solution)/shard_map/convert_element_type | solution.py:65
  (11 shorter events, 0.1 us)
Async XLA Ops:
  6.5 193.4 %all-gather.2.cloned.1.call-start = ((), (), s32[]{:S(2)}) async-start(), calls=%async_computation.1 | async-start | bytes 5308416 | tf_op jit(solution)/shard_map/all_gather | solution.py:48
  8.5 15.2 %collective-permute-start.1 = (bf16[64,4608]{1,0:T(8,128)(2,1)}, bf16[64,4608]{1,0:T(8,128)(2,1)S(1)}, u32[]{:S(2)}, u32[]{:S(2)}) collective-permute-start(bf16[64,4608]{1,0:T(8,128)(2,1)} %slice.23), channel_id=1, source_target_pairs={{0,32},{8,40},{16,48},{24,56},{32,0},{40,8},{48,16},{56,24},{64,96... | collective-permute-start | bytes 1769480 | tf_op jit(solution)/shard_map/ppermute | solution.py:18
  26.3 120.7 %copy-start.1 = (s32[1,256]{1,0:T(1,128)S(1)}, s32[1,256]{1,0:T(1,128)}, u32[]{:S(2)}) copy-start(s32[1,256]{1,0:T(1,128)} %param.8) | copy-start | bytes 3076
  26.3 121.1 %copy-start = (bf16[1,64,512]{2,1,0:T(8,128)(2,1)S(1)}, bf16[1,64,512]{2,1,0:T(8,128)(2,1)}, u32[]{:S(2)}) copy-start(bf16[1,64,512]{2,1,0:T(8,128)(2,1)} %param.7) | copy-start | bytes 196612
  26.3 126.4 %copy-start.2 = (s32[1,9]{1,0:T(1,128)S(1)}, s32[1,9]{1,0:T(1,128)}, u32[]{:S(2)}) copy-start(s32[1,9]{1,0:T(1,128)} %param.9) | copy-start | bytes 112
  26.3 165.7 %all-to-all-start = ((bf16[8,64,4608]{2,1,0:T(8,128)(2,1)}), bf16[8,64,4608]{2,1,0:T(8,128)(2,1)}, u32[]{:S(2)}, u32[]{:S(2)}) async-start(bf16[8,64,4608]{2,1,0:T(8,128)(2,1)} %stack.2), calls=%async_computation | async-start | bytes 9437184 | tf_op jit(solution)/shard_map/all_to_all | solution.py:13
  145.4 44.6 %collective-permute-start = (bf16[512,512]{0,1:T(8,128)(2,1)S(1)}, bf16[512,512]{0,1:T(8,128)(2,1)S(1)}, u32[]{:S(2)}, u32[]{:S(2)}) collective-permute-start(bf16[512,512]{0,1:T(8,128)(2,1)S(1)} %copy.17), channel_id=1, source_target_pairs={{0,32},{8,40},{16,48},{24,56},{32,0},{40,8},{48,16},{56,24},{64,96... | collective-permute-start | bytes 1572872 | tf_op jit(solution)/shard_map/ppermute | solution.py:18
Sparse Core Ops, SparseCore 0:
  9.6 117.3 all-gather.1
